TPU v7x, 32 devices: a whole 2x2x4 slice. The times are simulated.
32 devices in a mesh: dp: 4 (over x, core), ctx: 2 (over y), tensor: 4 (over z).
Axes of the slice: x: 2, y: 2, z: 4, core: 2. Of those that a mesh axis runs over, the one named last changes fastest.
Arguments:
- hidden_in: bfloat16 [8, 1024, 2048], P('dp', 'ctx'), may hold values from -36.5 to 36.5
- lengths: int32 [8], replicated, may hold values from 256 to 1024, as said below
- w_query: bfloat16 [2048, 2048], P(('dp', 'ctx'), 'tensor'), may hold values from -0.125 to 0.125
- w_keyval: bfloat16 [2048, 4, 128], P(('dp', 'ctx'), 'tensor'), may hold values from -0.125 to 0.125
- w_output: bfloat16 [2048, 2048], P(('dp', 'ctx'), 'tensor'), may hold values from -1.5 to 1.5
- w_gateup: bfloat16 [2048, 2, 5632], P(('dp', 'ctx'), None, 'tensor'), may hold values from -0.125 to 0.125
- w_down: bfloat16 [2048, 5632], P(('dp', 'ctx'), 'tensor'), may hold values from -0.078125 to 0.078125
- gain_attn: bfloat16 [2048], P(('dp', 'ctx')), may hold values from 0.5 to 1.5
- gain_mlp: bfloat16 [2048], P(('dp', 'ctx')), may hold values from 0.5 to 1.5
- cotangent: bfloat16 [8, 1024, 2048], P('dp', 'ctx'), may hold values from -6 to 6
Outputs:
- output: bfloat16 [8, 1024, 2048], P('dp', 'ctx')
- input_grad: bfloat16 [8, 1024, 2048], P('dp', 'ctx')
- grad_query: float32 [2048, 2048], P(('dp', 'ctx'), 'tensor')
- grad_keyval: float32 [2048, 4, 128], P(('dp', 'ctx'), 'tensor')
- grad_output: float32 [2048, 2048], P(('dp', 'ctx'), 'tensor')
- grad_gateup: float32 [2048, 2, 5632], P(('dp', 'ctx'), None, 'tensor')
- grad_down: float32 [2048, 5632], P(('dp', 'ctx'), 'tensor')
- grad_gain_attn: float32 [2048], P(('dp', 'ctx'))
- grad_gain_mlp: float32 [2048], P(('dp', 'ctx'))
- root_means: float32 [3], replicated
Inputs may be any that keep to these rules, and one draw needn't show every extreme that they name: `lengths`: in every draw the first slot has exactly 1024 valid tokens and the last exactly 256.
All inputs are finite; a program needn't handle non-finite values.
Results may differ from a plain program's by a relative error of at most 0.014.
Values may be sent and summed in bfloat16 or wider, within the bound.
No kernel may reach another device: no remote copies, remote signals or barrier semaphores. Data moves between devices by JAX's collectives and lax.ppermute only.
A program may use at most 384 MiB of HBM per device.

v0:
```python
import jax
import jax.numpy as jnp
from jax import lax
from jax.sharding import PartitionSpec as P

D = 2048
HD = 64
EPS = 1e-05
THETA = 10000.0
NEG_FILL = -1e30


def from_behind(block, axis, distance):
    devices = range(lax.axis_size(axis))
    route = [(i - distance, i) for i in devices if i - distance in devices]
    return lax.ppermute(block, axis, route)


def rms_scale(values):
    return lax.rsqrt(jnp.mean(values * values, axis=-1, keepdims=True) + EPS)


def rope_tables(positions, head_width):
    frequency = THETA ** (-jnp.arange(0, head_width, 2).astype(jnp.float32) / head_width)
    angles = positions.astype(jnp.float32)[:, None] * frequency[None, :]
    angles = jnp.concatenate([angles, angles], axis=-1)
    return (jnp.cos(angles), jnp.sin(angles))


def rotate(values, cosine, sine):
    half_width = values.shape[-1] // 2
    turned = jnp.concatenate([-values[..., half_width:], values[..., :half_width]], axis=-1)
    return values * cosine + turned * sine


def rotate_back(grads, cosine, sine):
    half_width = grads.shape[-1] // 2
    scaled = grads * sine
    turned = jnp.concatenate([scaled[..., half_width:], -scaled[..., :half_width]], axis=-1)
    return grads * cosine + turned


def contract_rows(left, right):
    return lax.dot_general(
        left, right, (((0,), (0,)), ((), ())), preferred_element_type=jnp.float32
    )


def contract_cols(left, right):
    return lax.dot_general(
        left, right, (((1,), (1,)), ((), ())), preferred_element_type=jnp.float32
    )


def score_block(queries, pair, positions, key_positions, length):
    allowed = (
        (key_positions[None, :] <= positions[:, None])
        & (key_positions[None, :] >= 0)
        & (key_positions[None, :] < length)
    )
    raw_scores = jnp.einsum(
        "qhd,pd->hqp", queries, pair[:, :HD], preferred_element_type=jnp.float32
    )
    return jnp.where(allowed[None], raw_scores * HD ** (-0.5), NEG_FILL)


def forward_step(weights, positions, key_positions, cosine, sine, squares, packed):
    query_w, keyval_w, output_w, gateup_w, down_w, attn_gain, mlp_gain = weights
    token_rows, length = packed
    tokens = token_rows.astype(jnp.float32)
    rows, width = tokens.shape
    heads = query_w.shape[1] // HD
    live_mask = (positions < length).astype(jnp.float32)[:, None]
    normed = (tokens * rms_scale(tokens) * attn_gain.astype(jnp.float32)).astype(jnp.bfloat16)
    query_lin = jnp.dot(normed, query_w, preferred_element_type=jnp.float32)
    keyval_lin = jnp.dot(normed, keyval_w.reshape(width, -1), preferred_element_type=jnp.float32)
    queries = rotate(
        query_lin.reshape(rows, heads, HD), cosine[:, None, :], sine[:, None, :]
    ).astype(jnp.bfloat16)
    keys = rotate(keyval_lin[:, :HD], cosine, sine)
    local_pair = jnp.concatenate([keys, keyval_lin[:, HD:]], axis=-1).astype(jnp.bfloat16)
    remote_pair = from_behind(local_pair, "ctx", 1)
    pair = jnp.concatenate([remote_pair, local_pair], axis=0)
    scores = score_block(queries, pair, positions, key_positions, length)
    top = jnp.max(scores, axis=-1, keepdims=True)
    shifted = jnp.exp(scores - top)
    total = jnp.sum(shifted, axis=-1, keepdims=True)
    attend = (shifted / total).astype(jnp.bfloat16)
    log_total = top + jnp.log(total)
    context = jnp.einsum("hqp,pd->qhd", attend, pair[:, HD:], preferred_element_type=jnp.float32)
    context = context.reshape(rows, heads * HD).astype(jnp.bfloat16)
    attn_part = contract_cols(context, output_w)
    attn_out = lax.psum(attn_part, "tensor")
    middle = tokens + attn_out
    normed_mlp = (middle * rms_scale(middle) * mlp_gain.astype(jnp.float32)).astype(jnp.bfloat16)
    gateup = jnp.dot(
        normed_mlp, gateup_w.reshape(width, -1), preferred_element_type=jnp.float32
    ).reshape(rows, 2, -1)
    hidden = (jax.nn.silu(gateup[:, 0]) * gateup[:, 1]).astype(jnp.bfloat16)
    mlp_part = contract_cols(hidden, down_w)
    mlp_out = lax.psum(mlp_part.astype(jnp.bfloat16), "tensor").astype(jnp.float32)
    result = (middle + mlp_out) * live_mask
    squares = squares + jnp.stack(
        [
            jnp.sum(result * result),
            jnp.sum(attn_out * attn_out * live_mask),
            jnp.sum(mlp_out * mlp_out * live_mask),
        ]
    )
    saved = (normed, queries, pair, log_total, context, middle, normed_mlp, gateup)
    return (squares, (result.astype(jnp.bfloat16), saved))


def backward_step(weights, positions, key_positions, cosine, sine, totals, packed):
    query_w, keyval_w, output_w, gateup_w, down_w, attn_gain, mlp_gain = weights
    token_rows, seed_rows, length, saved = packed
    normed, queries, pair, log_total, context, middle, normed_mlp, gateup = saved
    tokens = token_rows.astype(jnp.float32)
    rows, width = tokens.shape
    heads = queries.shape[1]
    live_mask = (positions < length).astype(jnp.float32)[:, None]
    seed = seed_rows.astype(jnp.float32) * live_mask
    mlp_seed = seed.astype(jnp.bfloat16)
    gate_lin = gateup[:, 0]
    up_lin = gateup[:, 1]
    sigmoid_gate = jax.nn.sigmoid(gate_lin)
    activated = jax.nn.silu(gate_lin)
    hidden = (activated * up_lin).astype(jnp.bfloat16)
    grad_hidden = jnp.dot(mlp_seed, down_w, preferred_element_type=jnp.float32)
    grad_gate = grad_hidden * up_lin * (sigmoid_gate * (1.0 + gate_lin * (1.0 - sigmoid_gate)))
    grad_up = grad_hidden * activated
    grad_gateup = jnp.stack([grad_gate, grad_up], axis=1).reshape(rows, -1).astype(jnp.bfloat16)
    gateup_flat = gateup_w.reshape(width, -1)
    mlp_back_part = contract_cols(grad_gateup, gateup_flat)
    grad_normed_mlp = lax.psum(mlp_back_part, "tensor")
    mlp_scale = rms_scale(middle)
    weighted_mlp = grad_normed_mlp * mlp_gain.astype(jnp.float32)
    grad_middle = (
        seed
        + mlp_scale * weighted_mlp
        - middle * mlp_scale**3 * jnp.mean(weighted_mlp * middle, axis=-1, keepdims=True)
    )
    seed_part_low = grad_middle.astype(jnp.bfloat16)
    grad_context = (
        jnp.dot(seed_part_low, output_w, preferred_element_type=jnp.float32)
        .astype(jnp.bfloat16)
        .reshape(rows, heads, HD)
    )
    scores = score_block(queries, pair, positions, key_positions, length)
    attend_full = jnp.exp(scores - log_total)
    grad_attend = jnp.einsum(
        "qhd,pd->hqp", grad_context, pair[:, HD:], preferred_element_type=jnp.float32
    )
    center = jnp.sum(attend_full * grad_attend, axis=-1, keepdims=True)
    grad_raw = (attend_full * (grad_attend - center) * HD ** (-0.5)).astype(jnp.bfloat16)
    grad_values = jnp.einsum(
        "hqp,qhd->pd",
        attend_full.astype(jnp.bfloat16),
        grad_context,
        preferred_element_type=jnp.float32,
    )
    grad_queries = jnp.einsum(
        "hqp,pd->qhd", grad_raw, pair[:, :HD], preferred_element_type=jnp.float32
    )
    grad_keys = jnp.einsum("hqp,qhd->pd", grad_raw, queries, preferred_element_type=jnp.float32)
    grad_pair = jnp.concatenate([grad_keys, grad_values], axis=-1)
    returned = from_behind(grad_pair[:rows], "ctx", -1)
    grad_own = grad_pair[rows:] + returned
    grad_keyval = jnp.concatenate(
        [rotate_back(grad_own[:, :HD], cosine, sine), grad_own[:, HD:]], axis=-1
    ).astype(jnp.bfloat16)
    grad_query_lin = (
        rotate_back(grad_queries, cosine[:, None, :], sine[:, None, :])
        .reshape(rows, -1)
        .astype(jnp.bfloat16)
    )
    keyval_flat = keyval_w.reshape(width, -1)
    attn_back_part = contract_cols(grad_query_lin, query_w) + contract_cols(
        grad_keyval, keyval_flat
    )
    grad_normed = lax.psum(attn_back_part, "tensor")
    attn_scale = rms_scale(tokens)
    weighted_attn = grad_normed * attn_gain.astype(jnp.float32)
    grad_tokens = (
        grad_middle
        + attn_scale * weighted_attn
        - tokens * attn_scale**3 * jnp.mean(weighted_attn * tokens, axis=-1, keepdims=True)
    )
    updates = (
        contract_rows(normed, grad_query_lin),
        contract_rows(normed, grad_keyval).reshape(keyval_w.shape),
        contract_rows(seed_part_low, context),
        contract_rows(normed_mlp, grad_gateup).reshape(gateup_w.shape),
        contract_rows(mlp_seed, hidden),
        jnp.sum(grad_normed * tokens * attn_scale, axis=0),
        jnp.sum(grad_normed_mlp * middle * mlp_scale, axis=0),
    )
    totals = tuple((running + extra for running, extra in zip(totals, updates)))
    return (totals, grad_tokens.astype(jnp.bfloat16))


def body(
    hidden_in,
    lengths,
    w_query,
    w_keyval,
    w_output,
    w_gateup,
    w_down,
    gain_attn,
    gain_mlp,
    cotangent,
):
    micro, rows, width = hidden_in.shape
    positions = lax.axis_index("ctx") * rows + jnp.arange(rows, dtype=jnp.int32)
    key_positions = jnp.concatenate([positions - rows, positions])
    cosine, sine = rope_tables(positions, HD)
    slot_lengths = lax.dynamic_slice_in_dim(lengths, lax.axis_index("dp") * micro, micro)
    shards = (w_query, w_keyval, w_output, w_gateup, w_down, gain_attn, gain_mlp)

    def forward_fn(squares, packed):
        fresh = (
            lax.all_gather(w_query, ("dp", "ctx"), axis=0, tiled=True),
            lax.all_gather(w_keyval, ("dp", "ctx"), axis=0, tiled=True),
            lax.all_gather(w_output, ("dp", "ctx"), axis=0, tiled=True),
            lax.all_gather(w_gateup, ("dp", "ctx"), axis=0, tiled=True),
            lax.all_gather(w_down, ("dp", "ctx"), axis=0, tiled=True),
            lax.all_gather(gain_attn, ("dp", "ctx"), axis=0, tiled=True),
            lax.all_gather(gain_mlp, ("dp", "ctx"), axis=0, tiled=True),
        )
        return forward_step(fresh, positions, key_positions, cosine, sine, squares, packed)

    def backward_fn(totals, packed):
        fresh = (
            lax.all_gather(w_query, ("dp", "ctx"), axis=0, tiled=True),
            lax.all_gather(w_keyval, ("dp", "ctx"), axis=0, tiled=True),
            lax.all_gather(w_output, ("dp", "ctx"), axis=0, tiled=True),
            lax.all_gather(w_gateup, ("dp", "ctx"), axis=0, tiled=True),
            lax.all_gather(w_down, ("dp", "ctx"), axis=0, tiled=True),
            lax.all_gather(gain_attn, ("dp", "ctx"), axis=0, tiled=True),
            lax.all_gather(gain_mlp, ("dp", "ctx"), axis=0, tiled=True),
        )
        return backward_step(fresh, positions, key_positions, cosine, sine, totals, packed)

    squares, (results, saved) = lax.scan(
        forward_fn, jnp.zeros((3,), jnp.float32), (hidden_in, slot_lengths)
    )
    empty_totals = tuple((jnp.zeros((D,) + shard.shape[1:], jnp.float32) for shard in shards))
    totals, grad_rows = lax.scan(
        backward_fn, empty_totals, (hidden_in, cotangent, slot_lengths, saved)
    )
    square_totals = lax.psum(squares, ("dp", "ctx"))
    valid_count = jnp.sum(lengths).astype(jnp.float32) * D
    root_means = jnp.sqrt(square_totals / valid_count)
    reduced = (
        lax.psum_scatter(totals[0], ("dp", "ctx"), scatter_dimension=0, tiled=True),
        lax.psum_scatter(totals[1], ("dp", "ctx"), scatter_dimension=0, tiled=True),
        lax.psum_scatter(totals[2], ("dp", "ctx"), scatter_dimension=0, tiled=True),
        lax.psum_scatter(totals[3], ("dp", "ctx"), scatter_dimension=0, tiled=True),
        lax.psum_scatter(totals[4], ("dp", "ctx"), scatter_dimension=0, tiled=True),
        lax.psum_scatter(totals[5], ("dp", "ctx"), scatter_dimension=0, tiled=True),
        lax.psum_scatter(totals[6], ("dp", "ctx"), scatter_dimension=0, tiled=True),
    )
    return (
        results,
        grad_rows,
        reduced[0],
        reduced[1],
        reduced[2],
        reduced[3],
        reduced[4],
        reduced[5],
        reduced[6],
        root_means,
    )


def solution(mesh):
    placed = (
        P("dp", "ctx", None),
        P(),
        P(("dp", "ctx"), "tensor"),
        P(("dp", "ctx"), "tensor", None),
        P(("dp", "ctx"), "tensor"),
        P(("dp", "ctx"), None, "tensor"),
        P(("dp", "ctx"), "tensor"),
        P(("dp", "ctx")),
        P(("dp", "ctx")),
        P("dp", "ctx", None),
    )
    return jax.shard_map(
        body,
        mesh=mesh,
        in_specs=placed,
        out_specs=(
            P("dp", "ctx", None),
            P("dp", "ctx", None),
            P(("dp", "ctx"), "tensor"),
            P(("dp", "ctx"), "tensor", None),
            P(("dp", "ctx"), "tensor"),
            P(("dp", "ctx"), None, "tensor"),
            P(("dp", "ctx"), "tensor"),
            P(("dp", "ctx")),
            P(("dp", "ctx")),
            P(),
        ),
        check_vma=False,
    )
```

profile of v0, /device:TPU:0, one launch (start us, length us, event | category | flops | bytes accessed | tf_op | source)
XLA Modules:
  0.0 2640.3 jit_solution(12595167485632672327)
XLA Ops:
  20.6 915.7 %while.54 = (s32[]{:T(128)}, f32[3]{0:T(128)S(1)}, bf16[2,512,2048]{2,1,0:T(8,128)(2,1)}, bf16[2,512,2048]{2,1,0:T(8,128)(2,1)}, bf16[2,512,8,64]{1,3,2,0:T(8,12...) while((s32[]{:T(128)}, f32[3]{0:T(128)S(1)}, ...), condition=%wide.region_10.11_spmd.clone, body=%wide.region_0.10_spmd.clone.sunk | while | flops 12453074944 | bytes 434036544 | solution.py:245
  22.1 14.2 all-gather.12
  38.3 19.8 all_gather.63
  103.7 13.9 all-gather.13
  117.7 140.5 %all-reduce.12.cloned.1.call-done = f32[512,2048]{1,0:T(8,128)} async-done(((f32[512,2048]{1,0:T(8,128)}), f32[512,2048]{1,0:T(8,128)}) %all-reduce.12.cloned.1.call-update) | async-done | bytes 4194320 | tf_op jit(solution)/shard_map/while/body/eval_jaxpr/psum | solution.py:93
  266.8 59.9 %all-gather.31.cloned.1.call-done = bf16[2048,2,1408]{2,1,0:T(2,128)(2,1)} async-done(((bf16[256,2,1408]{2,1,0:T(2,128)(2,1)}), bf16[2048,2,1408]{2,1,0:T(2,128)(2,1)}) %all-gather.31.cloned.1.call-update) | async-done | bytes 11534352 | tf_op jit(solution)/shard_map/while/body/eval_jaxpr/all_gather | solution.py:226
  350.2 12.8 fusion.236
  402.2 65.4 %all-reduce.14.cloned.1.call-done = bf16[512,2048]{1,0:T(8,128)(2,1)} async-done(((bf16[512,2048]{1,0:T(8,128)(2,1)}), bf16[512,2048]{1,0:T(8,128)(2,1)}) %all-reduce.14.cloned.1.call-update) | async-done | bytes 2097168 | tf_op jit(solution)/shard_map/while/body/eval_jaxpr/psum | solution.py:101
  481.4 13.0 all-gather.12
  496.5 18.0 all_gather.63
  560.9 14.6 all-gather.13
  575.6 138.7 %all-reduce.12.cloned.1.call-done = f32[512,2048]{1,0:T(8,128)} async-done(((f32[512,2048]{1,0:T(8,128)}), f32[512,2048]{1,0:T(8,128)}) %all-reduce.12.cloned.1.call-update) | async-done | bytes 4194320 | tf_op jit(solution)/shard_map/while/body/eval_jaxpr/psum | solution.py:93
  722.9 59.9 %all-gather.31.cloned.1.call-done = bf16[2048,2,1408]{2,1,0:T(2,128)(2,1)} async-done(((bf16[256,2,1408]{2,1,0:T(2,128)(2,1)}), bf16[2048,2,1408]{2,1,0:T(2,128)(2,1)}) %all-gather.31.cloned.1.call-update) | async-done | bytes 11534352 | tf_op jit(solution)/shard_map/while/body/eval_jaxpr/all_gather | solution.py:226
  806.4 12.8 fusion.236
  858.5 65.3 %all-reduce.14.cloned.1.call-done = bf16[512,2048]{1,0:T(8,128)(2,1)} async-done(((bf16[512,2048]{1,0:T(8,128)(2,1)}), bf16[512,2048]{1,0:T(8,128)(2,1)}) %all-reduce.14.cloned.1.call-update) | async-done | bytes 2097168 | tf_op jit(solution)/shard_map/while/body/eval_jaxpr/psum | solution.py:101
  938.8 1127.0 %while.55 = (s32[]{:T(128)}, f32[2048,512]{1,0:T(8,128)}, f32[2048,1,128]{2,0,1:T(8,128)}, f32[2048,512]{1,0:T(8,128)}, f32[2048,2,1408]{2,0,1:T(8,128)}, /*inde...) while((s32[]{:T(128)}, f32[2048,512]{1,0:T(8,128)}, ...), condition=%wide.region_21.22_spmd.clone, body=%wide.region_11.21_spmd.clone.sunk | while | flops 25381644288 | bytes 722071680 | solution.py:249
  955.7 35.1 %all-gather.37.cloned.1.call-done = bf16[2048,1408]{1,0:T(8,128)(2,1)} async-done(((bf16[256,1408]{1,0:T(8,128)(2,1)}), bf16[2048,1408]{1,0:T(8,128)(2,1)}) %all-gather.37.cloned.1.call-update) | async-done | bytes 5767184 | tf_op jit(solution)/shard_map/while/body/eval_jaxpr/all_gather | solution.py:239
  1001.0 60.0 %all-gather.35.cloned.1.call-done = bf16[2048,2,1408]{2,0,1:T(8,128)(2,1)} async-done(((bf16[256,2,1408]{2,0,1:T(8,128)(2,1)}), bf16[2048,2,1408]{2,0,1:T(8,128)(2,1)}) %all-gather.35.cloned.1.call-update) | async-done | bytes 11534352 | tf_op jit(solution)/shard_map/while/body/eval_jaxpr/all_gather | solution.py:238
  1061.0 10.8 convolution_bitcast_fusion.3
  1076.4 13.6 all-gather.14
  1090.0 18.4 all_gather.71
  1117.4 109.6 %all-reduce.16.cloned.1.call-done = f32[512,2048]{1,0:T(8,128)} async-done(((f32[512,2048]{1,0:T(8,128)}), f32[512,2048]{1,0:T(8,128)}) %all-reduce.16.cloned.1.call-update) | async-done | bytes 4194320 | tf_op jit(solution)/shard_map/while/body/eval_jaxpr/psum | solution.py:135
  1237.6 18.1 all-gather.33.cloned.1.call-done
  1268.1 22.3 fusion.269
  1300.7 26.5 %broadcast_multiply_fusion.8 = (f32[512,8,64]{0,2,1:T(8,128)}, f32[512,8,64]{0,2,1:T(8,128)}) fusion(f32[512,64]{0,1:T(8,128)} %copy-done.17, f32[8,512,1024]{1,2,0:T(8,128)} %fusion.260, f32[1024,512,8]{1,0,2:T(8,128)} %fusion.265, bf16[1024,128]{0,1:T(8,128)(2,1)S(1)} %dynamic-slice_bitcast_fusion.5), kind=kOutput, calls=%fused_computation.172.clone.1 | convolution fusion | flops 558109696 | bytes 69468160 | tf_op jit(solution)/shard_map/while/body/eval_jaxpr/hqp,pd->qhd/dot_general | solution.py:162
  1336.9 11.4 select_add_fusion.15
  1348.3 14.8 all-gather.15
  1370.6 13.1 select_add_fusion.14
  1394.4 99.7 %all-reduce.18.cloned.1.call-done = f32[512,2048]{1,0:T(8,128)} async-done(((f32[512,2048]{1,0:T(8,128)}), f32[512,2048]{1,0:T(8,128)}) %all-reduce.18.cloned.1.call-update) | async-done | bytes 4194320 | tf_op jit(solution)/shard_map/while/body/eval_jaxpr/psum | solution.py:181
  1514.2 35.1 %all-gather.37.cloned.1.call-done = bf16[2048,1408]{1,0:T(8,128)(2,1)} async-done(((bf16[256,1408]{1,0:T(8,128)(2,1)}), bf16[2048,1408]{1,0:T(8,128)(2,1)}) %all-gather.37.cloned.1.call-update) | async-done | bytes 5767184 | tf_op jit(solution)/shard_map/while/body/eval_jaxpr/all_gather | solution.py:239
  1559.5 60.0 %all-gather.35.cloned.1.call-done = bf16[2048,2,1408]{2,0,1:T(8,128)(2,1)} async-done(((bf16[256,2,1408]{2,0,1:T(8,128)(2,1)}), bf16[2048,2,1408]{2,0,1:T(8,128)(2,1)}) %all-gather.35.cloned.1.call-update) | async-done | bytes 11534352 | tf_op jit(solution)/shard_map/while/body/eval_jaxpr/all_gather | solution.py:238
  1635.3 13.6 all-gather.14
  1648.9 18.5 all_gather.71
  1676.5 109.1 %all-reduce.16.cloned.1.call-done = f32[512,2048]{1,0:T(8,128)} async-done(((f32[512,2048]{1,0:T(8,128)}), f32[512,2048]{1,0:T(8,128)}) %all-reduce.16.cloned.1.call-update) | async-done | bytes 4194320 | tf_op jit(solution)/shard_map/while/body/eval_jaxpr/psum | solution.py:135
  1796.2 18.3 all-gather.33.cloned.1.call-done
  1826.8 22.3 fusion.269
  1859.2 26.5 %broadcast_multiply_fusion.8 = (f32[512,8,64]{0,2,1:T(8,128)}, f32[512,8,64]{0,2,1:T(8,128)}) fusion(f32[512,64]{0,1:T(8,128)} %copy-done.17, f32[8,512,1024]{1,2,0:T(8,128)} %fusion.260, f32[1024,512,8]{1,0,2:T(8,128)} %fusion.265, bf16[1024,128]{0,1:T(8,128)(2,1)S(1)} %dynamic-slice_bitcast_fusion.5), kind=kOutput, calls=%fused_computation.172.clone.1 | convolution fusion | flops 558109696 | bytes 69468160 | tf_op jit(solution)/shard_map/while/body/eval_jaxpr/hqp,pd->qhd/dot_general | solution.py:162
  1895.4 14.5 select_add_fusion.15
  1909.8 15.1 all-gather.15
  1932.4 16.7 select_add_fusion.14
  1960.9 91.7 %all-reduce.18.cloned.1.call-done = f32[512,2048]{1,0:T(8,128)} async-done(((f32[512,2048]{1,0:T(8,128)}), f32[512,2048]{1,0:T(8,128)}) %all-reduce.18.cloned.1.call-update) | async-done | bytes 4194320 | tf_op jit(solution)/shard_map/while/body/eval_jaxpr/psum | solution.py:181
  2065.9 38.7 %copy.57 = f32[2048,2,1408]{2,1,0:T(2,128)} copy(f32[2048,2,1408]{2,0,1:T(8,128)} %get-tuple-element.318) | data formatting | bytes 46137344 | tf_op jit(solution)/shard_map/while | solution.py:249
  2109.9 26.0 all-reduce.3
  2137.6 252.9 %all-reduce.10.cloned.1.call-done = f32[2048,2,1408]{2,1,0:T(2,128)} async-done(((f32[2048,2,1408]{2,1,0:T(2,128)}), f32[2048,2,1408]{2,1,0:T(2,128)}) %all-reduce.10.cloned.1.call-update) | async-done | bytes 23068688
  2394.9 35.5 %reduce-scatter.7.cloned.1.call-done = f32[256,1,128]{2,1,0:T(1,128)} async-done(((f32[2048,1,128]{2,1,0:T(1,128)}), f32[256,1,128]{2,1,0:T(1,128)}) %reduce-scatter.7.cloned.1.call-update) | async-done | bytes 131088 | tf_op jit(solution)/shard_map/reduce_scatter | solution.py:257
  2430.4 55.4 %reduce-scatter.5.cloned.1.call-done = f32[256,512]{1,0:T(8,128)} async-done(((f32[2048,512]{1,0:T(8,128)}), f32[256,512]{1,0:T(8,128)}) %reduce-scatter.5.cloned.1.call-update) | async-done | bytes 524304 | tf_op jit(solution)/shard_map/reduce_scatter | solution.py:256
  2485.8 55.2 %reduce-scatter.9.cloned.1.call-done = f32[256,512]{1,0:T(8,128)} async-done(((f32[2048,512]{1,0:T(8,128)}), f32[256,512]{1,0:T(8,128)}) %reduce-scatter.9.cloned.1.call-update) | async-done | bytes 524304 | tf_op jit(solution)/shard_map/reduce_scatter | solution.py:258
  2541.0 91.1 %reduce-scatter.11.cloned.1.call-done = f32[256,1408]{1,0:T(8,128)} async-done(((f32[2048,1408]{1,0:T(8,128)}), f32[256,1408]{1,0:T(8,128)}) %reduce-scatter.11.cloned.1.call-update) | async-done | bytes 1441808 | tf_op jit(solution)/shard_map/reduce_scatter | solution.py:260
  (458 shorter events, 511.9 us)
Async XLA Ops:
  20.6 46.2 %all-gather.25.cloned.1.call-start = ((), (), s32[]{:S(2)}) async-start(), calls=%async_computation.9 | async-start | bytes 2359296 | tf_op jit(solution)/shard_map/while/body/eval_jaxpr/all_gather | solution.py:223
  21.4 75.5 %all-gather.27.cloned.1.call-start = ((), (), s32[]{:S(2)}) async-start(), calls=%async_computation.10 | async-start | bytes 2359296 | tf_op jit(solution)/shard_map/while/body/eval_jaxpr/all_gather | solution.py:225
  60.8 6.0 collective-permute-start
  63.2 195.0 %all-reduce.12.cloned.1.call-start = ((), (), s32[]{:S(2)}) async-start(), calls=%async_computation.11 | async-start | bytes 8388608 | tf_op jit(solution)/shard_map/while/body/eval_jaxpr/psum | solution.py:93
  101.8 224.8 %all-gather.31.cloned.1.call-start = ((), (), s32[]{:S(2)}) async-start(), calls=%async_computation.13 | async-start | bytes 12976128 | tf_op jit(solution)/shard_map/while/body/eval_jaxpr/all_gather | solution.py:226
  102.4 269.3 %all-gather.29.cloned.1.call-start = ((), (), s32[]{:S(2)}) async-start(), calls=%async_computation.12 | async-start | bytes 6488064 | tf_op jit(solution)/shard_map/while/body/eval_jaxpr/all_gather | solution.py:227
  103.0 364.6 %all-reduce.14.cloned.1.call-start = ((), (), s32[]{:S(2)}) async-start(), calls=%async_computation.14 | async-start | bytes 4194304 | tf_op jit(solution)/shard_map/while/body/eval_jaxpr/psum | solution.py:101
  480.0 43.8 %all-gather.25.cloned.1.call-start = ((), (), s32[]{:S(2)}) async-start(), calls=%async_computation.9 | async-start | bytes 2359296 | tf_op jit(solution)/shard_map/while/body/eval_jaxpr/all_gather | solution.py:223
  480.7 73.2 %all-gather.27.cloned.1.call-start = ((), (), s32[]{:S(2)}) async-start(), calls=%async_computation.10 | async-start | bytes 2359296 | tf_op jit(solution)/shard_map/while/body/eval_jaxpr/all_gather | solution.py:225
  517.1 6.7 collective-permute-start
  520.7 193.6 %all-reduce.12.cloned.1.call-start = ((), (), s32[]{:S(2)}) async-start(), calls=%async_computation.11 | async-start | bytes 8388608 | tf_op jit(solution)/shard_map/while/body/eval_jaxpr/psum | solution.py:93
  558.9 223.9 %all-gather.31.cloned.1.call-start = ((), (), s32[]{:S(2)}) async-start(), calls=%async_computation.13 | async-start | bytes 12976128 | tf_op jit(solution)/shard_map/while/body/eval_jaxpr/all_gather | solution.py:226
  559.5 268.5 %all-gather.29.cloned.1.call-start = ((), (), s32[]{:S(2)}) async-start(), calls=%async_computation.12 | async-start | bytes 6488064 | tf_op jit(solution)/shard_map/while/body/eval_jaxpr/all_gather | solution.py:227
  560.2 363.6 %all-reduce.14.cloned.1.call-start = ((), (), s32[]{:S(2)}) async-start(), calls=%async_computation.14 | async-start | bytes 4194304 | tf_op jit(solution)/shard_map/while/body/eval_jaxpr/psum | solution.py:101
  945.6 388.4 %copy-start.10 = (f32[512,64]{0,1:T(8,128)}, f32[512,64]{0,1:T(8,128)S(1)}, u32[]{:S(2)}) copy-start(f32[512,64]{0,1:T(8,128)S(1)} %get-tuple-element.1391) | copy-start | bytes 393220 | tf_op jit(solution)/shard_map/while
  945.6 45.2 %all-gather.37.cloned.1.call-start = ((), (), s32[]{:S(2)}) async-start(), calls=%async_computation.17 | async-start | bytes 6488064 | tf_op jit(solution)/shard_map/while/body/eval_jaxpr/all_gather | solution.py:239
  946.3 114.6 %all-gather.35.cloned.1.call-start = ((), (), s32[]{:S(2)}) async-start(), calls=%async_computation.16 | async-start | bytes 12976128 | tf_op jit(solution)/shard_map/while/body/eval_jaxpr/all_gather | solution.py:238
  946.9 280.1 %all-reduce.16.cloned.1.call-start = ((), (), s32[]{:S(2)}) async-start(), calls=%async_computation.18 | async-start | bytes 8388608 | tf_op jit(solution)/shard_map/while/body/eval_jaxpr/psum | solution.py:135
  1001.0 70.9 %copy-start.16 = (bf16[512,1,1408]{2,0,1:T(8,128)(2,1)}, bf16[512,1,1408]{2,0,1:T(8,128)(2,1)S(1)}, u32[]{:S(2)}) copy-start(bf16[512,1,1408]{2,0,1:T(8,128)(2,1)S(1)} %get-tuple-element.1210) | copy-start | bytes 4325380 | tf_op jit(solution)/shard_map/while
  1071.9 37.4 %copy-start.41 = (bf16[2,512,8,64]{1,3,2,0:T(8,128)(2,1)S(1)}, bf16[2,512,8,64]{1,3,2,0:T(8,128)(2,1)}, u32[]{:S(2)}) copy-start(bf16[2,512,8,64]{1,3,2,0:T(8,128)(2,1)} %get-tuple-element.1382) | copy-start | bytes 3145732 | tf_op jit(solution)/shard_map/while
  1071.9 183.8 %all-gather.33.cloned.1.call-start = ((), (), s32[]{:S(2)}) async-start(), calls=%async_computation.15 | async-start | bytes 2359296 | tf_op jit(solution)/shard_map/while/body/eval_jaxpr/all_gather | solution.py:237
  1072.5 257.5 %all-gather.39.cloned.1.call-start = ((), (), s32[]{:S(2)}) async-start(), calls=%async_computation.19 | async-start | bytes 2359296 | tf_op jit(solution)/shard_map/while/body/eval_jaxpr/all_gather | solution.py:235
  1073.1 421.0 %all-reduce.18.cloned.1.call-start = ((), (), s32[]{:S(2)}) async-start(), calls=%async_computation.20 | async-start | bytes 8388608 | tf_op jit(solution)/shard_map/while/body/eval_jaxpr/psum | solution.py:181
  1299.0 34.0 %collective-permute-start.1 = (f32[512,128]{0,1:T(8,128)S(1)}, f32[512,128]{0,1:T(8,128)S(1)}, u32[]{:S(2)}, u32[]{:S(2)}) collective-permute-start(f32[512,128]{0,1:T(8,128)S(1)} %pad_maximum_fusion.13), channel_id=1, source_target_pairs={{4,0},{5,1},{6,2},{7,3},{12,8},{13,9},{14,10},{15,11},{20,16},{21,... | collective-permute-start | bytes 786440 | tf_op jit(solution)/shard_map/while/body/eval_jaxpr/ppermute | solution.py:16
  1393.3 100.8 %copy-start.30 = (f32[512]{0:T(512)S(1)}, f32[512]{0:T(512)}, u32[]{:S(2)}) copy-start(f32[512]{0:T(512)} %get-tuple-element.1220) | copy-start | bytes 6148 | tf_op jit(solution)/shard_map/while
  1394.4 109.4 %copy-start.15 = (f32[2048,1,128]{2,0,1:T(8,128)}, f32[2048,1,128]{2,0,1:T(8,128)S(1)}, u32[]{:S(2)}) copy-start(f32[2048,1,128]{2,0,1:T(8,128)S(1)} %fusion.273) | copy-start | bytes 3145732 | tf_op jit(solution)/shard_map/while
  1394.4 104.0 %copy-start.34 = (f32[2048]{0:T(1024)S(1)}, f32[2048]{0:T(1024)}, u32[]{:S(2)}) copy-start(f32[2048]{0:T(1024)} %get-tuple-element.1342) | copy-start | bytes 24580 | tf_op jit(solution)/shard_map/while
  1394.4 104.0 %copy-start.37 = (f32[512]{0:T(512)S(1)}, f32[512]{0:T(512)}, u32[]{:S(2)}) copy-start(f32[512]{0:T(512)} %get-tuple-element.1224) | copy-start | bytes 6148 | tf_op jit(solution)/shard_map/while
  1504.1 388.4 %copy-start.10 = (f32[512,64]{0,1:T(8,128)}, f32[512,64]{0,1:T(8,128)S(1)}, u32[]{:S(2)}) copy-start(f32[512,64]{0,1:T(8,128)S(1)} %get-tuple-element.1391) | copy-start | bytes 393220 | tf_op jit(solution)/shard_map/while
  1504.1 45.2 %all-gather.37.cloned.1.call-start = ((), (), s32[]{:S(2)}) async-start(), calls=%async_computation.17 | async-start | bytes 6488064 | tf_op jit(solution)/shard_map/while/body/eval_jaxpr/all_gather | solution.py:239
  1504.9 114.7 %all-gather.35.cloned.1.call-start = ((), (), s32[]{:S(2)}) async-start(), calls=%async_computation.16 | async-start | bytes 12976128 | tf_op jit(solution)/shard_map/while/body/eval_jaxpr/all_gather | solution.py:238
  1505.5 280.1 %all-reduce.16.cloned.1.call-start = ((), (), s32[]{:S(2)}) async-start(), calls=%async_computation.18 | async-start | bytes 8388608 | tf_op jit(solution)/shard_map/while/body/eval_jaxpr/psum | solution.py:135
  1559.5 70.9 %copy-start.16 = (bf16[512,1,1408]{2,0,1:T(8,128)(2,1)}, bf16[512,1,1408]{2,0,1:T(8,128)(2,1)S(1)}, u32[]{:S(2)}) copy-start(bf16[512,1,1408]{2,0,1:T(8,128)(2,1)S(1)} %get-tuple-element.1210) | copy-start | bytes 4325380 | tf_op jit(solution)/shard_map/while
  1630.4 18.5 copy-start.24
  1630.5 37.9 %copy-start.41 = (bf16[2,512,8,64]{1,3,2,0:T(8,128)(2,1)S(1)}, bf16[2,512,8,64]{1,3,2,0:T(8,128)(2,1)}, u32[]{:S(2)}) copy-start(bf16[2,512,8,64]{1,3,2,0:T(8,128)(2,1)} %get-tuple-element.1382) | copy-start | bytes 3145732 | tf_op jit(solution)/shard_map/while
  1630.5 184.0 %all-gather.33.cloned.1.call-start = ((), (), s32[]{:S(2)}) async-start(), calls=%async_computation.15 | async-start | bytes 2359296 | tf_op jit(solution)/shard_map/while/body/eval_jaxpr/all_gather | solution.py:237
  1631.2 257.3 %all-gather.39.cloned.1.call-start = ((), (), s32[]{:S(2)}) async-start(), calls=%async_computation.19 | async-start | bytes 2359296 | tf_op jit(solution)/shard_map/while/body/eval_jaxpr/all_gather | solution.py:235
  1632.0 420.6 %all-reduce.18.cloned.1.call-start = ((), (), s32[]{:S(2)}) async-start(), calls=%async_computation.20 | async-start | bytes 8388608 | tf_op jit(solution)/shard_map/while/body/eval_jaxpr/psum | solution.py:181
  1857.7 33.8 %collective-permute-start.1 = (f32[512,128]{0,1:T(8,128)S(1)}, f32[512,128]{0,1:T(8,128)S(1)}, u32[]{:S(2)}, u32[]{:S(2)}) collective-permute-start(f32[512,128]{0,1:T(8,128)S(1)} %pad_maximum_fusion.13), channel_id=1, source_target_pairs={{4,0},{5,1},{6,2},{7,3},{12,8},{13,9},{14,10},{15,11},{20,16},{21,... | collective-permute-start | bytes 786440 | tf_op jit(solution)/shard_map/while/body/eval_jaxpr/ppermute | solution.py:16
  1959.8 92.8 %copy-start.30 = (f32[512]{0:T(512)S(1)}, f32[512]{0:T(512)}, u32[]{:S(2)}) copy-start(f32[512]{0:T(512)} %get-tuple-element.1220) | copy-start | bytes 6148 | tf_op jit(solution)/shard_map/while
  1960.8 101.5 %copy-start.15 = (f32[2048,1,128]{2,0,1:T(8,128)}, f32[2048,1,128]{2,0,1:T(8,128)S(1)}, u32[]{:S(2)}) copy-start(f32[2048,1,128]{2,0,1:T(8,128)S(1)} %fusion.273) | copy-start | bytes 3145732 | tf_op jit(solution)/shard_map/while
  1960.9 96.0 %copy-start.34 = (f32[2048]{0:T(1024)S(1)}, f32[2048]{0:T(1024)}, u32[]{:S(2)}) copy-start(f32[2048]{0:T(1024)} %get-tuple-element.1342) | copy-start | bytes 24580 | tf_op jit(solution)/shard_map/while
  1960.9 96.0 %copy-start.37 = (f32[512]{0:T(512)S(1)}, f32[512]{0:T(512)}, u32[]{:S(2)}) copy-start(f32[512]{0:T(512)} %get-tuple-element.1224) | copy-start | bytes 6148 | tf_op jit(solution)/shard_map/while
  2065.9 324.7 %all-reduce.10.cloned.1.call-start = ((), (), s32[]{:S(2)}) async-start(), calls=%async_computation.8 | async-start | bytes 46137344
  2104.6 325.8 %reduce-scatter.7.cloned.1.call-start = ((), (), s32[]{:S(2)}) async-start(), calls=%async_computation.5 | async-start | bytes 1179648 | tf_op jit(solution)/shard_map/reduce_scatter | solution.py:257
  2105.2 380.6 %reduce-scatter.5.cloned.1.call-start = ((), (), s32[]{:S(2)}) async-start(), calls=%async_computation.4 | async-start | bytes 4718592 | tf_op jit(solution)/shard_map/reduce_scatter | solution.py:256
  2105.8 435.2 %reduce-scatter.9.cloned.1.call-start = ((), (), s32[]{:S(2)}) async-start(), calls=%async_computation.6 | async-start | bytes 4718592 | tf_op jit(solution)/shard_map/reduce_scatter | solution.py:258
  2106.5 525.6 %reduce-scatter.11.cloned.1.call-start = ((), (), s32[]{:S(2)}) async-start(), calls=%async_computation.7 | async-start | bytes 12976128 | tf_op jit(solution)/shard_map/reduce_scatter | solution.py:260
  (75 other events, 465.2 us)
Sparse Core Ops, SparseCore 0:
  24.1 32.3 all-gather.24
  63.3 27.7 all-gather.26
  101.9 156.1 all-reduce.11
  259.9 66.6 all-gather.30
  328.4 43.3 all-gather.28
  381.0 86.4 all-reduce.13
  483.4 27.5 all-gather.24
  520.8 26.1 all-gather.26
  559.0 155.2 all-reduce.11
  716.0 66.6 all-gather.30
  784.6 43.3 all-gather.28
  837.3 86.4 all-reduce.13
  948.5 42.2 all-gather.36
  993.3 67.6 all-gather.34
  1072.0 154.9 all-reduce.15
  1228.8 26.8 all-gather.32
  1257.4 27.9 all-gather.38
  1337.0 157.0 all-reduce.17
  1507.0 42.3 all-gather.36
  1551.8 67.6 all-gather.34
  1630.6 154.9 all-reduce.15
  1787.5 26.8 all-gather.32
  1816.3 27.9 all-gather.38
  1895.5 157.0 all-reduce.17
Sparse Core Ops, SparseCore 1:
  2104.7 285.7 all-reduce.9
  2394.5 35.9 reduce-scatter.6
  2434.6 51.2 reduce-scatter.4
  2489.8 51.2 reduce-scatter.8
  2545.5 86.6 reduce-scatter.10
where the time goes:
time: 2660 us; the launch traced here: 2640 us
  waiting for transfers between devices  1690 us (64%)
  matrix products  371 us (14%)
  blocking collectives  213 us (8%)
  local copies, waits for them, and re-layouts  190 us (7%)
  other arithmetic  140 us (5%)
    psum x2, waiting for transfers between devices, forward_step(): attn_out = lax.psum(attn_part, 'tensor')  279 us
    unnamed x6, waiting for transfers between devices  255 us
    psum x2, waiting for transfers between devices, backward_step(): grad_normed_mlp = lax.psum(mlp_back_part, 'tensor')  219 us
    psum x2, waiting for transfers between devices, backward_step(): grad_normed = lax.psum(attn_back_part, 'tensor')  191 us
    psum x2, waiting for transfers between devices, forward_step(): lax.psum(mlp_part.astype(jnp.bfloat16), 'tensor').astype(jnp.float32)  131 us
    all_gather x2, waiting for transfers between devices, backward_fn(): lax.all_gather(w_gateup, ('dp', 'ctx'), axis=0, tiled=True)  120 us
    all_gather x2, waiting for transfers between devices, forward_fn(): lax.all_gather(w_gateup, ('dp', 'ctx'), axis=0, tiled=True)  120 us
    reduce_scatter x1, waiting for transfers between devices, body(): lax.psum_scatter(totals[4], ('dp', 'ctx'), scatter_dimension=0, tiled=True)  91.1 us
  transfers between devices with their start and end apart: 33, of which 25 were waited for; matrix products, arithmetic and copies ran while one was open for 20% of the time, Pallas kernels for 0%

commit v1 on v0

--- a/solution.py
+++ b/solution.py
@@ -178,7 +178,19 @@
     attn_back_part = contract_cols(grad_query_lin, query_w) + contract_cols(
         grad_keyval, keyval_flat
     )
-    grad_normed = lax.psum(attn_back_part, "tensor")
+
+    def _pass_stacks_all(inputs):
+        devs = lax.psum(1, axis_name="tensor")
+        inter = inputs
+        for j in [
+            [(it, it ^ hop_no) for it in range(devs)]
+            for hop_no in (1, 2, 4, 8, 16)
+            if hop_no < devs
+        ]:
+            inter = inter + lax.ppermute(inter, axis_name="tensor", perm=j)
+        return inter
+
+    grad_normed = _pass_stacks_all(attn_back_part)
     attn_scale = rms_scale(tokens)
     weighted_attn = grad_normed * attn_gain.astype(jnp.float32)
     grad_tokens = (

time: 2660 us -> 2920 us (1.098)
  waiting for transfers between devices: 1690 us -> 1940 us
    ppermute x0 -> x4, waiting for transfers between devices: none -> 438 us  [_pass_stacks_all(): inter = inter + lax.ppermute(inter, axis_name='tensor', perm=j)]
    psum x2 -> x0, waiting for transfers between devices: 191 us -> none  [backward_step(): grad_normed = lax.psum(attn_back_part, 'tensor')]
  transfers between devices with their start and end apart: 33 -> 35, of which waited for: 25 -> 27; matrix products, arithmetic and copies ran while one was open for 20% -> 18% of each run, Pallas kernels for 0% -> 0%
where the time goes in v1:
time: 2920 us; the launch traced here: 2900 us
  waiting for transfers between devices  1940 us (66%)
  matrix products  361 us (12%)
  blocking collectives  211 us (7%)
  local copies, waits for them, and re-layouts  190 us (7%)
  other arithmetic  152 us (5%)
    ppermute x4, waiting for transfers between devices, _pass_stacks_all(): inter = inter + lax.ppermute(inter, axis_name='tensor', perm=j)  438 us
    psum x2, waiting for transfers between devices, forward_step(): attn_out = lax.psum(attn_part, 'tensor')  279 us
    unnamed x6, waiting for transfers between devices  258 us
    psum x2, waiting for transfers between devices, backward_step(): grad_normed_mlp = lax.psum(mlp_back_part, 'tensor')  219 us
    psum x2, waiting for transfers between devices, forward_step(): lax.psum(mlp_part.astype(jnp.bfloat16), 'tensor').astype(jnp.float32)  131 us
    all_gather x2, waiting for transfers between devices, backward_fn(): lax.all_gather(w_gateup, ('dp', 'ctx'), axis=0, tiled=True)  120 us
    all_gather x2, waiting for transfers between devices, forward_fn(): lax.all_gather(w_gateup, ('dp', 'ctx'), axis=0, tiled=True)  120 us
    reduce_scatter x1, waiting for transfers between devices, body(): lax.psum_scatter(totals[4], ('dp', 'ctx'), scatter_dimension=0, tiled=True)  91.1 us
  transfers between devices with their start and end apart: 35, of which 27 were waited for; matrix products, arithmetic and copies ran while one was open for 18% of the time, Pallas kernels for 0%

profile of v1, /device:TPU:0, one launch (start us, length us, event | category | flops | bytes accessed | tf_op | source)
XLA Modules:
  0.0 2899.4 jit_solution(17960184575818893438)
XLA Ops:
  20.6 915.4 %while.54 = (s32[]{:T(128)}, f32[3]{0:T(128)S(1)}, bf16[2,512,2048]{2,1,0:T(8,128)(2,1)}, bf16[2,512,2048]{2,1,0:T(8,128)(2,1)}, bf16[2,512,8,64]{1,3,2,0:T(8,12...) while((s32[]{:T(128)}, f32[3]{0:T(128)S(1)}, ...), condition=%wide.region_10.11_spmd.clone, body=%wide.region_0.10_spmd.clone.sunk | while | flops 12453074944 | bytes 434036544 | solution.py:257
  22.0 14.2 all-gather.12
  38.3 19.8 all_gather.63
  103.6 14.0 all-gather.13
  117.6 140.5 %all-reduce.11.cloned.1.call-done = f32[512,2048]{1,0:T(8,128)} async-done(((f32[512,2048]{1,0:T(8,128)}), f32[512,2048]{1,0:T(8,128)}) %all-reduce.11.cloned.1.call-update) | async-done | bytes 4194320 | tf_op jit(solution)/shard_map/while/body/eval_jaxpr/psum | solution.py:93
  266.7 59.9 %all-gather.31.cloned.1.call-done = bf16[2048,2,1408]{2,1,0:T(2,128)(2,1)} async-done(((bf16[256,2,1408]{2,1,0:T(2,128)(2,1)}), bf16[2048,2,1408]{2,1,0:T(2,128)(2,1)}) %all-gather.31.cloned.1.call-update) | async-done | bytes 11534352 | tf_op jit(solution)/shard_map/while/body/eval_jaxpr/all_gather | solution.py:238
  350.2 12.7 fusion.236
  402.1 65.4 %all-reduce.13.cloned.1.call-done = bf16[512,2048]{1,0:T(8,128)(2,1)} async-done(((bf16[512,2048]{1,0:T(8,128)(2,1)}), bf16[512,2048]{1,0:T(8,128)(2,1)}) %all-reduce.13.cloned.1.call-update) | async-done | bytes 2097168 | tf_op jit(solution)/shard_map/while/body/eval_jaxpr/psum | solution.py:101
  481.3 13.0 all-gather.12
  496.3 18.0 all_gather.63
  560.8 14.6 all-gather.13
  575.4 138.7 %all-reduce.11.cloned.1.call-done = f32[512,2048]{1,0:T(8,128)} async-done(((f32[512,2048]{1,0:T(8,128)}), f32[512,2048]{1,0:T(8,128)}) %all-reduce.11.cloned.1.call-update) | async-done | bytes 4194320 | tf_op jit(solution)/shard_map/while/body/eval_jaxpr/psum | solution.py:93
  722.7 59.8 %all-gather.31.cloned.1.call-done = bf16[2048,2,1408]{2,1,0:T(2,128)(2,1)} async-done(((bf16[256,2,1408]{2,1,0:T(2,128)(2,1)}), bf16[2048,2,1408]{2,1,0:T(2,128)(2,1)}) %all-gather.31.cloned.1.call-update) | async-done | bytes 11534352 | tf_op jit(solution)/shard_map/while/body/eval_jaxpr/all_gather | solution.py:238
  806.1 12.7 fusion.236
  858.3 65.3 %all-reduce.13.cloned.1.call-done = bf16[512,2048]{1,0:T(8,128)(2,1)} async-done(((bf16[512,2048]{1,0:T(8,128)(2,1)}), bf16[512,2048]{1,0:T(8,128)(2,1)}) %all-reduce.13.cloned.1.call-update) | async-done | bytes 2097168 | tf_op jit(solution)/shard_map/while/body/eval_jaxpr/psum | solution.py:101
  938.5 1384.0 %while.55 = (s32[]{:T(128)}, f32[2048,512]{1,0:T(8,128)}, f32[2048,1,128]{2,0,1:T(8,128)}, f32[2048,512]{1,0:T(8,128)}, f32[2048,2,1408]{2,0,1:T(8,128)}, /*inde...) while((s32[]{:T(128)}, f32[2048,512]{1,0:T(8,128)}, ...), condition=%wide.region_20.21_spmd.clone, body=%wide.region_11.20_spmd.clone.sunk | while | flops 25383741440 | bytes 819064960 | solution.py:261
  955.4 35.1 %all-gather.37.cloned.1.call-done = bf16[2048,1408]{1,0:T(8,128)(2,1)} async-done(((bf16[256,1408]{1,0:T(8,128)(2,1)}), bf16[2048,1408]{1,0:T(8,128)(2,1)}) %all-gather.37.cloned.1.call-update) | async-done | bytes 5767184 | tf_op jit(solution)/shard_map/while/body/eval_jaxpr/all_gather | solution.py:251
  1000.6 60.0 %all-gather.35.cloned.1.call-done = bf16[2048,2,1408]{2,0,1:T(8,128)(2,1)} async-done(((bf16[256,2,1408]{2,0,1:T(8,128)(2,1)}), bf16[2048,2,1408]{2,0,1:T(8,128)(2,1)}) %all-gather.35.cloned.1.call-update) | async-done | bytes 11534352 | tf_op jit(solution)/shard_map/while/body/eval_jaxpr/all_gather | solution.py:250
  1075.9 13.6 all-gather.14
  1089.5 18.3 all_gather.71
  1116.8 109.8 %all-reduce.15.cloned.1.call-done = f32[512,2048]{1,0:T(8,128)} async-done(((f32[512,2048]{1,0:T(8,128)}), f32[512,2048]{1,0:T(8,128)}) %all-reduce.15.cloned.1.call-update) | async-done | bytes 4194320 | tf_op jit(solution)/shard_map/while/body/eval_jaxpr/psum | solution.py:135
  1237.1 18.1 all-gather.33.cloned.1.call-done
  1267.6 22.3 fusion.269
  1300.2 26.7 broadcast_multiply_fusion.8
  1338.1 91.6 %collective-permute-done.2 = f32[512,2048]{1,0:T(8,128)} collective-permute-done((f32[512,2048]{1,0:T(8,128)}, f32[512,2048]{1,0:T(8,128)}, u32[]{:S(2)}, u32[]{:S(2)}) %collective-permute-start.2) | collective-permute-done | bytes 4194336 | tf_op jit(solution)/shard_map/while/body/eval_jaxpr/ppermute | solution.py:190
  1445.3 13.6 all-gather.15
  1466.5 13.1 select_add_fusion.14
  1488.4 130.9 %collective-permute-done.3 = f32[512,2048]{1,0:T(8,128)} collective-permute-done((f32[512,2048]{1,0:T(8,128)}, f32[512,2048]{1,0:T(8,128)}, u32[]{:S(2)}, u32[]{:S(2)}) %collective-permute-start.3) | collective-permute-done | bytes 4194336 | tf_op jit(solution)/shard_map/while/body/eval_jaxpr/ppermute | solution.py:190
  1641.2 37.3 %all-gather.37.cloned.1.call-done = bf16[2048,1408]{1,0:T(8,128)(2,1)} async-done(((bf16[256,1408]{1,0:T(8,128)(2,1)}), bf16[2048,1408]{1,0:T(8,128)(2,1)}) %all-gather.37.cloned.1.call-update) | async-done | bytes 5767184 | tf_op jit(solution)/shard_map/while/body/eval_jaxpr/all_gather | solution.py:251
  1688.7 60.2 %all-gather.35.cloned.1.call-done = bf16[2048,2,1408]{2,0,1:T(8,128)(2,1)} async-done(((bf16[256,2,1408]{2,0,1:T(8,128)(2,1)}), bf16[2048,2,1408]{2,0,1:T(8,128)(2,1)}) %all-gather.35.cloned.1.call-update) | async-done | bytes 11534352 | tf_op jit(solution)/shard_map/while/body/eval_jaxpr/all_gather | solution.py:250
  1748.9 10.7 convolution_bitcast_fusion.3
  1764.4 13.6 all-gather.14
  1778.1 18.5 all_gather.71
  1805.6 109.2 %all-reduce.15.cloned.1.call-done = f32[512,2048]{1,0:T(8,128)} async-done(((f32[512,2048]{1,0:T(8,128)}), f32[512,2048]{1,0:T(8,128)}) %all-reduce.15.cloned.1.call-update) | async-done | bytes 4194320 | tf_op jit(solution)/shard_map/while/body/eval_jaxpr/psum | solution.py:135
  1925.3 18.3 all-gather.33.cloned.1.call-done
  1956.0 22.3 fusion.269
  1988.4 26.7 broadcast_multiply_fusion.8
  2026.2 91.6 %collective-permute-done.2 = f32[512,2048]{1,0:T(8,128)} collective-permute-done((f32[512,2048]{1,0:T(8,128)}, f32[512,2048]{1,0:T(8,128)}, u32[]{:S(2)}, u32[]{:S(2)}) %collective-permute-start.2) | collective-permute-done | bytes 4194336 | tf_op jit(solution)/shard_map/while/body/eval_jaxpr/ppermute | solution.py:190
  2136.1 13.7 all-gather.15
  2157.3 16.5 select_add_fusion.14
  2183.9 123.5 %collective-permute-done.3 = f32[512,2048]{1,0:T(8,128)} collective-permute-done((f32[512,2048]{1,0:T(8,128)}, f32[512,2048]{1,0:T(8,128)}, u32[]{:S(2)}, u32[]{:S(2)}) %collective-permute-start.3) | collective-permute-done | bytes 4194336 | tf_op jit(solution)/shard_map/while/body/eval_jaxpr/ppermute | solution.py:190
  2322.6 38.7 %copy.57 = f32[2048,2,1408]{2,1,0:T(2,128)} copy(f32[2048,2,1408]{2,0,1:T(8,128)} %get-tuple-element.318) | data formatting | bytes 46137344 | tf_op jit(solution)/shard_map/while | solution.py:261
  2366.5 26.0 all-reduce.3
  2394.3 255.4 %all-reduce.9.cloned.1.call-done = f32[2048,2,1408]{2,1,0:T(2,128)} async-done(((f32[2048,2,1408]{2,1,0:T(2,128)}), f32[2048,2,1408]{2,1,0:T(2,128)}) %all-reduce.9.cloned.1.call-update) | async-done | bytes 23068688
  2654.0 35.5 %reduce-scatter.7.cloned.1.call-done = f32[256,1,128]{2,1,0:T(1,128)} async-done(((f32[2048,1,128]{2,1,0:T(1,128)}), f32[256,1,128]{2,1,0:T(1,128)}) %reduce-scatter.7.cloned.1.call-update) | async-done | bytes 131088 | tf_op jit(solution)/shard_map/reduce_scatter | solution.py:269
  2689.5 55.4 %reduce-scatter.5.cloned.1.call-done = f32[256,512]{1,0:T(8,128)} async-done(((f32[2048,512]{1,0:T(8,128)}), f32[256,512]{1,0:T(8,128)}) %reduce-scatter.5.cloned.1.call-update) | async-done | bytes 524304 | tf_op jit(solution)/shard_map/reduce_scatter | solution.py:268
  2744.9 55.2 %reduce-scatter.9.cloned.1.call-done = f32[256,512]{1,0:T(8,128)} async-done(((f32[2048,512]{1,0:T(8,128)}), f32[256,512]{1,0:T(8,128)}) %reduce-scatter.9.cloned.1.call-update) | async-done | bytes 524304 | tf_op jit(solution)/shard_map/reduce_scatter | solution.py:270
  2800.1 91.1 %reduce-scatter.11.cloned.1.call-done = f32[256,1408]{1,0:T(8,128)} async-done(((f32[2048,1408]{1,0:T(8,128)}), f32[256,1408]{1,0:T(8,128)}) %reduce-scatter.11.cloned.1.call-update) | async-done | bytes 1441808 | tf_op jit(solution)/shard_map/reduce_scatter | solution.py:272
  (484 shorter events, 548.3 us)
Async XLA Ops:
  20.6 46.2 %all-gather.25.cloned.1.call-start = ((), (), s32[]{:S(2)}) async-start(), calls=%async_computation.9 | async-start | bytes 2359296 | tf_op jit(solution)/shard_map/while/body/eval_jaxpr/all_gather | solution.py:235
  21.3 75.5 %all-gather.27.cloned.1.call-start = ((), (), s32[]{:S(2)}) async-start(), calls=%async_computation.10 | async-start | bytes 2359296 | tf_op jit(solution)/shard_map/while/body/eval_jaxpr/all_gather | solution.py:237
  60.8 6.0 collective-permute-start
  63.2 194.9 %all-reduce.11.cloned.1.call-start = ((), (), s32[]{:S(2)}) async-start(), calls=%async_computation.11 | async-start | bytes 8388608 | tf_op jit(solution)/shard_map/while/body/eval_jaxpr/psum | solution.py:93
  101.8 224.8 %all-gather.31.cloned.1.call-start = ((), (), s32[]{:S(2)}) async-start(), calls=%async_computation.13 | async-start | bytes 12976128 | tf_op jit(solution)/shard_map/while/body/eval_jaxpr/all_gather | solution.py:238
  102.3 269.3 %all-gather.29.cloned.1.call-start = ((), (), s32[]{:S(2)}) async-start(), calls=%async_computation.12 | async-start | bytes 6488064 | tf_op jit(solution)/shard_map/while/body/eval_jaxpr/all_gather | solution.py:239
  102.9 364.5 %all-reduce.13.cloned.1.call-start = ((), (), s32[]{:S(2)}) async-start(), calls=%async_computation.14 | async-start | bytes 4194304 | tf_op jit(solution)/shard_map/while/body/eval_jaxpr/psum | solution.py:101
  479.8 43.8 %all-gather.25.cloned.1.call-start = ((), (), s32[]{:S(2)}) async-start(), calls=%async_computation.9 | async-start | bytes 2359296 | tf_op jit(solution)/shard_map/while/body/eval_jaxpr/all_gather | solution.py:235
  480.6 73.2 %all-gather.27.cloned.1.call-start = ((), (), s32[]{:S(2)}) async-start(), calls=%async_computation.10 | async-start | bytes 2359296 | tf_op jit(solution)/shard_map/while/body/eval_jaxpr/all_gather | solution.py:237
  517.0 6.7 collective-permute-start
  520.5 193.5 %all-reduce.11.cloned.1.call-start = ((), (), s32[]{:S(2)}) async-start(), calls=%async_computation.11 | async-start | bytes 8388608 | tf_op jit(solution)/shard_map/while/body/eval_jaxpr/psum | solution.py:93
  558.7 223.8 %all-gather.31.cloned.1.call-start = ((), (), s32[]{:S(2)}) async-start(), calls=%async_computation.13 | async-start | bytes 12976128 | tf_op jit(solution)/shard_map/while/body/eval_jaxpr/all_gather | solution.py:238
  559.3 268.5 %all-gather.29.cloned.1.call-start = ((), (), s32[]{:S(2)}) async-start(), calls=%async_computation.12 | async-start | bytes 6488064 | tf_op jit(solution)/shard_map/while/body/eval_jaxpr/all_gather | solution.py:239
  560.0 363.6 %all-reduce.13.cloned.1.call-start = ((), (), s32[]{:S(2)}) async-start(), calls=%async_computation.14 | async-start | bytes 4194304 | tf_op jit(solution)/shard_map/while/body/eval_jaxpr/psum | solution.py:101
  945.2 388.5 %copy-start.10 = (f32[512,64]{0,1:T(8,128)}, f32[512,64]{0,1:T(8,128)S(1)}, u32[]{:S(2)}) copy-start(f32[512,64]{0,1:T(8,128)S(1)} %get-tuple-element.1391) | copy-start | bytes 393220 | tf_op jit(solution)/shard_map/while
  945.2 45.2 %all-gather.37.cloned.1.call-start = ((), (), s32[]{:S(2)}) async-start(), calls=%async_computation.17 | async-start | bytes 6488064 | tf_op jit(solution)/shard_map/while/body/eval_jaxpr/all_gather | solution.py:251
  946.0 114.6 %all-gather.35.cloned.1.call-start = ((), (), s32[]{:S(2)}) async-start(), calls=%async_computation.16 | async-start | bytes 12976128 | tf_op jit(solution)/shard_map/while/body/eval_jaxpr/all_gather | solution.py:250
  946.6 280.0 %all-reduce.15.cloned.1.call-start = ((), (), s32[]{:S(2)}) async-start(), calls=%async_computation.18 | async-start | bytes 8388608 | tf_op jit(solution)/shard_map/while/body/eval_jaxpr/psum | solution.py:135
  1071.4 183.8 %all-gather.33.cloned.1.call-start = ((), (), s32[]{:S(2)}) async-start(), calls=%async_computation.15 | async-start | bytes 2359296 | tf_op jit(solution)/shard_map/while/body/eval_jaxpr/all_gather | solution.py:249
  1072.0 257.7 %all-gather.39.cloned.1.call-start = ((), (), s32[]{:S(2)}) async-start(), calls=%async_computation.19 | async-start | bytes 2359296 | tf_op jit(solution)/shard_map/while/body/eval_jaxpr/all_gather | solution.py:247
  1298.5 34.2 %collective-permute-start.1 = (f32[512,128]{0,1:T(8,128)S(1)}, f32[512,128]{0,1:T(8,128)S(1)}, u32[]{:S(2)}, u32[]{:S(2)}) collective-permute-start(f32[512,128]{0,1:T(8,128)S(1)} %pad_maximum_fusion.13), channel_id=1, source_target_pairs={{4,0},{5,1},{6,2},{7,3},{12,8},{13,9},{14,10},{15,11},{20,16},{21,... | collective-permute-start | bytes 786440 | tf_op jit(solution)/shard_map/while/body/eval_jaxpr/ppermute | solution.py:16
  1336.6 93.1 %collective-permute-start.2 = (f32[512,2048]{1,0:T(8,128)}, f32[512,2048]{1,0:T(8,128)}, u32[]{:S(2)}, u32[]{:S(2)}) collective-permute-start(f32[512,2048]{1,0:T(8,128)} %convolution_add_fusion.2), channel_id=1, source_target_pairs={{0,1},{1,0},{2,3},{3,2},{4,5},{5,4},{6,7},{7,6},{8,9},{9,8},{10,11... | collective-permute-start | bytes 12582920 | tf_op jit(solution)/shard_map/while/body/eval_jaxpr/ppermute | solution.py:190
  1338.1 100.6 %slice-start.1 = ((s8[5767168]{0:T(1024)(128)(4,1)}), s8[4194304]{0:T(1024)(128)(4,1)S(1)}, s32[]{:S(2)}) async-start(s8[5767168]{0:T(1024)(128)(4,1)} %bitcast.444), calls=%async_computation.21 | async-start | bytes 8388608 | tf_op jit(solution)/shard_map/while
  1338.1 100.6 %copy-start.20 = (bf16[2,512,2048]{2,1,0:T(8,128)(2,1)S(1)}, bf16[2,512,2048]{2,1,0:T(8,128)(2,1)}, u32[]{:S(2)}) copy-start(bf16[2,512,2048]{2,1,0:T(8,128)(2,1)} %get-tuple-element.1384) | copy-start | bytes 12582916 | tf_op jit(solution)/shard_map/while
  1436.2 183.0 %collective-permute-start.3 = (f32[512,2048]{1,0:T(8,128)}, f32[512,2048]{1,0:T(8,128)}, u32[]{:S(2)}, u32[]{:S(2)}) collective-permute-start(f32[512,2048]{1,0:T(8,128)} %add.399), channel_id=1, source_target_pairs={{0,2},{1,3},{2,0},{3,1},{4,6},{5,7},{6,4},{7,5},{8,10},{9,11},{10,... | collective-permute-start | bytes 12582920 | tf_op jit(solution)/shard_map/while/body/eval_jaxpr/ppermute | solution.py:190
  1487.1 137.3 %copy-start.9 = (f32[2048,512]{1,0:T(8,128)}, f32[2048,512]{1,0:T(8,128)S(1)}, u32[]{:S(2)}) copy-start(f32[2048,512]{1,0:T(8,128)S(1)} %select_add_fusion.13) | copy-start | bytes 12582916 | tf_op jit(solution)/shard_map/while
  1487.1 132.1 %copy-start.3 = (bf16[2,512,2048]{2,1,0:T(8,128)(2,1)S(1)}, bf16[2,512,2048]{2,1,0:T(8,128)(2,1)}, u32[]{:S(2)}) copy-start(bf16[2,512,2048]{2,1,0:T(8,128)(2,1)} %get-tuple-element.1397) | copy-start | bytes 12582916 | tf_op jit(solution)/shard_map/while
  1487.1 132.1 %copy-start.33 = (f32[512]{0:T(512)S(1)}, f32[512]{0:T(512)}, u32[]{:S(2)}) copy-start(f32[512]{0:T(512)} %get-tuple-element.1220) | copy-start | bytes 6148 | tf_op jit(solution)/shard_map/while
  1488.4 136.0 %copy-start.15 = (f32[2048,1,128]{2,0,1:T(8,128)}, f32[2048,1,128]{2,0,1:T(8,128)S(1)}, u32[]{:S(2)}) copy-start(f32[2048,1,128]{2,0,1:T(8,128)S(1)} %fusion.273) | copy-start | bytes 3145732 | tf_op jit(solution)/shard_map/while
  1631.1 390.8 %copy-start.10 = (f32[512,64]{0,1:T(8,128)}, f32[512,64]{0,1:T(8,128)S(1)}, u32[]{:S(2)}) copy-start(f32[512,64]{0,1:T(8,128)S(1)} %get-tuple-element.1391) | copy-start | bytes 393220 | tf_op jit(solution)/shard_map/while
  1631.1 47.4 %all-gather.37.cloned.1.call-start = ((), (), s32[]{:S(2)}) async-start(), calls=%async_computation.17 | async-start | bytes 6488064 | tf_op jit(solution)/shard_map/while/body/eval_jaxpr/all_gather | solution.py:251
  1631.7 117.2 %all-gather.35.cloned.1.call-start = ((), (), s32[]{:S(2)}) async-start(), calls=%async_computation.16 | async-start | bytes 12976128 | tf_op jit(solution)/shard_map/while/body/eval_jaxpr/all_gather | solution.py:250
  1632.5 282.3 %all-reduce.15.cloned.1.call-start = ((), (), s32[]{:S(2)}) async-start(), calls=%async_computation.18 | async-start | bytes 8388608 | tf_op jit(solution)/shard_map/while/body/eval_jaxpr/psum | solution.py:135
  1759.7 184.0 %all-gather.33.cloned.1.call-start = ((), (), s32[]{:S(2)}) async-start(), calls=%async_computation.15 | async-start | bytes 2359296 | tf_op jit(solution)/shard_map/while/body/eval_jaxpr/all_gather | solution.py:249
  1760.4 257.5 %all-gather.39.cloned.1.call-start = ((), (), s32[]{:S(2)}) async-start(), calls=%async_computation.19 | async-start | bytes 2359296 | tf_op jit(solution)/shard_map/while/body/eval_jaxpr/all_gather | solution.py:247
  1986.9 34.0 %collective-permute-start.1 = (f32[512,128]{0,1:T(8,128)S(1)}, f32[512,128]{0,1:T(8,128)S(1)}, u32[]{:S(2)}, u32[]{:S(2)}) collective-permute-start(f32[512,128]{0,1:T(8,128)S(1)} %pad_maximum_fusion.13), channel_id=1, source_target_pairs={{4,0},{5,1},{6,2},{7,3},{12,8},{13,9},{14,10},{15,11},{20,16},{21,... | collective-permute-start | bytes 786440 | tf_op jit(solution)/shard_map/while/body/eval_jaxpr/ppermute | solution.py:16
  2024.7 93.0 %collective-permute-start.2 = (f32[512,2048]{1,0:T(8,128)}, f32[512,2048]{1,0:T(8,128)}, u32[]{:S(2)}, u32[]{:S(2)}) collective-permute-start(f32[512,2048]{1,0:T(8,128)} %convolution_add_fusion.2), channel_id=1, source_target_pairs={{0,1},{1,0},{2,3},{3,2},{4,5},{5,4},{6,7},{7,6},{8,9},{9,8},{10,11... | collective-permute-start | bytes 12582920 | tf_op jit(solution)/shard_map/while/body/eval_jaxpr/ppermute | solution.py:190
  2026.2 100.6 %copy-start.20 = (bf16[2,512,2048]{2,1,0:T(8,128)(2,1)S(1)}, bf16[2,512,2048]{2,1,0:T(8,128)(2,1)}, u32[]{:S(2)}) copy-start(bf16[2,512,2048]{2,1,0:T(8,128)(2,1)} %get-tuple-element.1384) | copy-start | bytes 12582916 | tf_op jit(solution)/shard_map/while
  2124.4 183.0 %collective-permute-start.3 = (f32[512,2048]{1,0:T(8,128)}, f32[512,2048]{1,0:T(8,128)}, u32[]{:S(2)}, u32[]{:S(2)}) collective-permute-start(f32[512,2048]{1,0:T(8,128)} %add.399), channel_id=1, source_target_pairs={{0,2},{1,3},{2,0},{3,1},{4,6},{5,7},{6,4},{7,5},{8,10},{9,11},{10,... | collective-permute-start | bytes 12582920 | tf_op jit(solution)/shard_map/while/body/eval_jaxpr/ppermute | solution.py:190
  2182.6 129.9 %copy-start.9 = (f32[2048,512]{1,0:T(8,128)}, f32[2048,512]{1,0:T(8,128)S(1)}, u32[]{:S(2)}) copy-start(f32[2048,512]{1,0:T(8,128)S(1)} %select_add_fusion.13) | copy-start | bytes 12582916 | tf_op jit(solution)/shard_map/while
  2182.6 124.8 %copy-start.3 = (bf16[2,512,2048]{2,1,0:T(8,128)(2,1)S(1)}, bf16[2,512,2048]{2,1,0:T(8,128)(2,1)}, u32[]{:S(2)}) copy-start(bf16[2,512,2048]{2,1,0:T(8,128)(2,1)} %get-tuple-element.1397) | copy-start | bytes 12582916 | tf_op jit(solution)/shard_map/while
  2182.6 124.8 %copy-start.33 = (f32[512]{0:T(512)S(1)}, f32[512]{0:T(512)}, u32[]{:S(2)}) copy-start(f32[512]{0:T(512)} %get-tuple-element.1220) | copy-start | bytes 6148 | tf_op jit(solution)/shard_map/while
  2183.9 128.7 %copy-start.15 = (f32[2048,1,128]{2,0,1:T(8,128)}, f32[2048,1,128]{2,0,1:T(8,128)S(1)}, u32[]{:S(2)}) copy-start(f32[2048,1,128]{2,0,1:T(8,128)S(1)} %fusion.273) | copy-start | bytes 3145732 | tf_op jit(solution)/shard_map/while
  2322.5 327.1 %all-reduce.9.cloned.1.call-start = ((), (), s32[]{:S(2)}) async-start(), calls=%async_computation.8 | async-start | bytes 46137344
  2361.3 328.3 %reduce-scatter.7.cloned.1.call-start = ((), (), s32[]{:S(2)}) async-start(), calls=%async_computation.5 | async-start | bytes 1179648 | tf_op jit(solution)/shard_map/reduce_scatter | solution.py:269
  2361.8 383.1 %reduce-scatter.5.cloned.1.call-start = ((), (), s32[]{:S(2)}) async-start(), calls=%async_computation.4 | async-start | bytes 4718592 | tf_op jit(solution)/shard_map/reduce_scatter | solution.py:268
  2362.4 437.7 %reduce-scatter.9.cloned.1.call-start = ((), (), s32[]{:S(2)}) async-start(), calls=%async_computation.6 | async-start | bytes 4718592 | tf_op jit(solution)/shard_map/reduce_scatter | solution.py:270
  2363.2 528.1 %reduce-scatter.11.cloned.1.call-start = ((), (), s32[]{:S(2)}) async-start(), calls=%async_computation.7 | async-start | bytes 12976128 | tf_op jit(solution)/shard_map/reduce_scatter | solution.py:272
  (87 other events, 1011.5 us)
Sparse Core Ops, SparseCore 0:
  24.0 32.3 all-gather.24
  63.3 27.7 all-gather.26
  101.9 156.1 all-reduce.10
  259.8 66.6 all-gather.30
  328.3 43.3 all-gather.28
  380.9 86.4 all-reduce.12
  483.3 27.5 all-gather.24
  520.7 26.1 all-gather.26
  558.8 155.1 all-reduce.10
  715.8 66.6 all-gather.30
  784.4 43.3 all-gather.28
  837.1 86.4 all-reduce.12
  948.1 42.2 all-gather.36
  992.9 67.6 all-gather.34
  1071.5 154.9 all-reduce.14
  1228.3 26.8 all-gather.32
  1257.0 27.9 all-gather.38
  1633.7 44.7 all-gather.36
  1681.2 67.6 all-gather.34
  1759.8 154.9 all-reduce.14
  1916.7 26.8 all-gather.32
  1945.5 27.9 all-gather.38
Sparse Core Ops, SparseCore 1:
  2361.3 288.2 all-reduce.8
  2653.5 35.9 reduce-scatter.6
  2693.7 51.2 reduce-scatter.4
  2748.9 51.2 reduce-scatter.8
  2804.6 86.6 reduce-scatter.10
